TPU v7x, 32 devices: a whole 2x2x4 slice. The times are simulated.
32 devices in a mesh: clip: 2 (over x), space: 4 (over y, core), tm: 4 (over z).
Axes of the slice: x: 2, y: 2, z: 4, core: 2. Of those that a mesh axis runs over, the one named last changes fastest.
Arguments:
- block_input: bfloat16 [8, 12, 160, 384], P(('clip', 'tm'), 'space'), parts along dimension 0, may hold values from -24 to 24, as said below
- conv_input: bfloat16 [8, 12, 160, 384], P(('clip', 'tm'), 'space'), parts along dimension 0, may hold values from -24 to 24, as said below
- norm_gain: float32 [384], replicated, may hold values from 0.1 to 1.9
- norm_bias: float32 [384], replicated, may hold values from -3 to 3
- conv_weight: bfloat16 [3, 3, 3, 384, 384], replicated, may hold values from -0.0625 to 0.0625
- conv_bias: float32 [384], replicated, may hold values from -1.5 to 1.5
- attn_gain: float32 [384], replicated, may hold values from 0.1 to 1.9
- attn_bias: float32 [384], replicated, may hold values from -1.5 to 1.5
- query_weight: bfloat16 [384, 384], replicated, may hold values from -4 to 4
- query_bias: float32 [384], replicated, may hold values from -1.5 to 1.5
- key_weight: bfloat16 [384, 384], replicated, may hold values from -4 to 4
- value_weight: bfloat16 [384, 384], replicated, may hold values from -0.3125 to 0.3125
- value_bias: float32 [384], replicated, may hold values from -3 to 3
- out_weight: bfloat16 [384, 384], replicated, may hold values from -0.3125 to 0.3125
- out_bias: float32 [384], replicated, may hold values from -3 to 3
Outputs:
- block_output: bfloat16 [8, 12, 160, 384], P(('clip', 'tm'), 'space'), parts along dimension 0
There are 2 independent parts, one for each index of `clip`. A program takes and returns all parts, laid end to end along the dimension named above; an argument that names none is the same for every part. Nothing has to cross between parts.
Inputs may be any that keep to these rules, and one draw needn't show every extreme that they name: `block_input`: finite activations. `conv_input`: finite activations.
All inputs are finite; a program needn't handle non-finite values.
Results may differ from a plain program's by a relative error of at most 0.0075.
Values may be sent and summed in bfloat16 or wider, within the bound.
No kernel may reach another device: no remote copies, remote signals or barrier semaphores. Data moves between devices by JAX's collectives and lax.ppermute only.
A program may use at most 128 MiB of HBM per device.

v0:
```python
import jax
import jax.numpy as jnp
from jax import lax
from jax.sharding import PartitionSpec as P


def from_behind(value, axis, steps):
    count = lax.axis_size(axis)
    leading, last = (max(0, -steps), min(count, count - steps))
    return lax.ppermute(value, axis, [(source, source + steps) for source in range(leading, last)])


def padded_2(x, sides, width):
    for axis, dim in sides:
        peers, length = (lax.axis_size(axis), x.shape[dim])
        up = [(i, (i + 1) % peers) for i in range(peers - 1)]
        down = [(j, i) for i, j in up]
        last = lax.slice_in_dim(x, length - width, length, axis=dim)
        leading = lax.slice_in_dim(x, 0, width, axis=dim)
        before = lax.ppermute(last, axis, up)
        after = lax.ppermute(leading, axis, down)
        x = jnp.concatenate([before, x, after], axis=dim)
    return x


def rms_norm(field, gain, bias):
    mean_square = jnp.mean(field * field, axis=-1, keepdims=True)
    return field * lax.rsqrt(mean_square + 1e-06) * gain + bias


def causal_conv(padded, conv_weight, frame_count, row_count, columns):
    channels = padded.shape[-1]
    running = jnp.zeros((frame_count * row_count * columns, channels), jnp.float32)
    for tap_t in range(3):
        for tap_y in range(3):
            window = padded[tap_t : tap_t + frame_count, tap_y : tap_y + row_count]
            joined = jnp.concatenate(
                [window[:, :, tap_x : tap_x + columns] for tap_x in range(3)], axis=-1
            )
            joined = joined.reshape(-1, 3 * channels)
            kernel = conv_weight[tap_t, tap_y].reshape(3 * channels, channels)
            running = running + jnp.dot(joined, kernel, preferred_element_type=jnp.float32)
    return running.reshape(frame_count, row_count, columns, channels)


def absorb(state, queries, key_rows, value_rows, score_scale):
    numer_acc, denom_acc, max_acc = state
    scores = (
        jnp.einsum("fqc,fkc->fqk", queries, key_rows, preferred_element_type=jnp.float32)
        * score_scale
    )
    new_max = jnp.maximum(max_acc, jnp.max(scores, axis=-1))
    expd = jnp.exp(scores - new_max[..., None])
    weights = expd.astype(jnp.bfloat16)
    added = jnp.einsum("fqk,fkc->fqc", weights, value_rows, preferred_element_type=jnp.float32)
    numer_acc = added
    denom_acc = jnp.sum(expd, axis=-1)
    return (numer_acc, denom_acc, new_max)


def shards(
    block_input,
    conv_input,
    norm_gain,
    norm_bias,
    conv_weight,
    conv_bias,
    attn_gain,
    attn_bias,
    query_weight,
    query_bias,
    key_weight,
    value_weight,
    value_bias,
    out_weight,
    out_bias,
):
    frame_count, row_count, columns, channels = block_input.shape
    field = conv_input.astype(jnp.float32)
    activated = jax.nn.silu(rms_norm(field, norm_gain, norm_bias)).astype(jnp.bfloat16)
    earlier = [from_behind(activated, "tm", offset) for offset in (1, 2)]
    stacked = jnp.concatenate([earlier[1], earlier[0], activated], axis=0)
    padded = padded_2(stacked, (("space", 1),), 1)
    padded = jnp.pad(padded, ((0, 0), (0, 0), (1, 1), (0, 0)))
    convolved = causal_conv(padded, conv_weight, frame_count, row_count, columns) + conv_bias
    mixed = (block_input.astype(jnp.float32) + convolved).astype(jnp.bfloat16)
    mixed_wide = mixed.astype(jnp.float32)
    normed = rms_norm(mixed_wide, attn_gain, attn_bias).astype(jnp.bfloat16)
    flat_rows = normed.reshape(frame_count, row_count * columns, channels)
    score_scale = float(channels) ** (-0.5)
    queries = (
        jnp.dot(flat_rows, query_weight, preferred_element_type=jnp.float32) + query_bias
    ).astype(jnp.bfloat16)
    query_count = row_count * columns
    start_state = (
        jnp.zeros((frame_count, query_count, channels), jnp.float32),
        jnp.zeros((frame_count, query_count), jnp.float32),
        jnp.full((frame_count, query_count), -1e30, jnp.float32),
    )
    source = lax.all_gather(normed, "space", axis=1, tiled=True).reshape(frame_count, -1, channels)
    key_rows = jnp.dot(source, key_weight, preferred_element_type=jnp.float32).astype(jnp.bfloat16)
    value_rows = (
        jnp.dot(source, value_weight, preferred_element_type=jnp.float32) + value_bias
    ).astype(jnp.bfloat16)
    numer_acc, denom_acc, max_acc = absorb(start_state, queries, key_rows, value_rows, score_scale)
    attended = (numer_acc / denom_acc[..., None]).astype(jnp.bfloat16)
    projected = jnp.dot(attended, out_weight, preferred_element_type=jnp.float32) + out_bias
    return (mixed_wide + projected.reshape(mixed_wide.shape)).astype(jnp.bfloat16)


def solution(mesh):
    placed = (
        P(("clip", "tm"), "space", None, None),
        P(("clip", "tm"), "space", None, None),
        P(),
        P(),
        P(),
        P(),
        P(),
        P(),
        P(),
        P(),
        P(),
        P(),
        P(),
        P(),
        P(),
    )
    return jax.shard_map(
        shards,
        mesh=mesh,
        in_specs=placed,
        out_specs=P(("clip", "tm"), "space", None, None),
        check_vma=False,
    )
```

profile of v0, /device:TPU:0, one launch (start us, length us, event | category | flops | bytes accessed | tf_op | source)
XLA Modules:
  0.0 103.6 jit_solution(10755714841860632833)
XLA Ops:
  6.5 0.0 copy-start
  6.5 0.0 all-gather.2.cloned.1.call-start
  6.5 1.2 %fusion.35 = f32[3,160]{1,0:T(4,128)S(1)} fusion(bf16[1,3,160,384]{3,2,1,0:T(8,128)(2,1)} %param.16), kind=kLoop, calls=%fused_computation.72 | loop fusion | flops 552480 | bytes 370560 | tf_op jit(solution)/shard_map/reduce_sum | solution.py:27
  7.8 1.3 %fusion.43 = bf16[1,3,160,384]{3,2,1,0:T(8,128)(2,1)S(1)} fusion(bf16[1,3,160,384]{3,2,1,0:T(8,128)(2,1)} %param.16, f32[384]{0:T(512)} %param.18, f32[384]{0:T(512)} %param.17, f32[3,160]{1,0:T(4,128)S(1)} %add_rsqrt_fusion.1), kind=kLoop, calls=%fused_computation.80 | loop fusion | flops 1658880 | bytes 742272 | tf_op jit(solution)/shard_map/convert_element_type | solution.py:80
  9.1 5.0 %collective-permute-start.1 = (bf16[1,3,160,384]{3,2,1,0:T(8,128)(2,1)S(1)}, bf16[1,3,160,384]{3,2,1,0:T(8,128)(2,1)S(1)}, u32[]{:S(2)}, u32[]{:S(2)}) collective-permute-start(bf16[1,3,160,384]{3,2,1,0:T(8,128)(2,1)S(1)} %fusion.43), channel_id=1, source_target_pairs={{0,1},{1,2},{2,3},{4,5},{5,6},{6,7},{8,9},{9,10},{10,11},{12,13},{... | collective-permute-start | bytes 1105928 | tf_op jit(solution)/shard_map/ppermute | solution.py:10
  14.1 4.5 %collective-permute-start = (bf16[1,3,160,384]{3,2,1,0:T(8,128)(2,1)S(1)}, bf16[1,3,160,384]{3,2,1,0:T(8,128)(2,1)S(1)}, u32[]{:S(2)}, u32[]{:S(2)}) collective-permute-start(bf16[1,3,160,384]{3,2,1,0:T(8,128)(2,1)S(1)} %fusion.43), channel_id=1, source_target_pairs={{0,2},{1,3},{4,6},{5,7},{8,10},{9,11},{12,14},{13,15},{16,18},{17,... | collective-permute-start | bytes 1105928 | tf_op jit(solution)/shard_map/ppermute | solution.py:10
  18.6 4.4 %collective-permute-done.1 = bf16[1,3,160,384]{3,2,1,0:T(8,128)(2,1)S(1)} collective-permute-done((bf16[1,3,160,384]{3,2,1,0:T(8,128)(2,1)S(1)}, bf16[1,3,160,384]{3,2,1,0:T(8,128)(2,1)S(1)}, u32[]{:S(2)}, u32[]{:S(2)}) %collective-permute-start.1) | collective-permute-done | bytes 368672 | tf_op jit(solution)/shard_map/ppermute | solution.py:10
  23.0 6.8 %collective-permute-done = bf16[1,3,160,384]{3,2,1,0:T(8,128)(2,1)S(1)} collective-permute-done((bf16[1,3,160,384]{3,2,1,0:T(8,128)(2,1)S(1)}, bf16[1,3,160,384]{3,2,1,0:T(8,128)(2,1)S(1)}, u32[]{:S(2)}, u32[]{:S(2)}) %collective-permute-start) | collective-permute-done | bytes 368672 | tf_op jit(solution)/shard_map/ppermute | solution.py:10
  29.8 0.1 pad_maximum_fusion.21
  29.9 1.3 %collective-permute-start.2 = (bf16[3,1,160,384]{3,2,1,0:T(8,128)(2,1)S(1)}, bf16[3,1,160,384]{3,2,1,0:T(8,128)(2,1)S(1)}, u32[]{:S(2)}, u32[]{:S(2)}) collective-permute-start(bf16[3,1,160,384]{3,2,1,0:T(8,128)(2,1)S(1)} %get-tuple-element.41), channel_id=1, source_target_pairs={{0,4},{4,8},{8,12},{1,5},{5,9},{9,13},{2,6},{6,10},{10,14},{3,7},{... | collective-permute-start | bytes 1105928 | tf_op jit(solution)/shard_map/ppermute | solution.py:20
  31.3 1.3 %collective-permute-start.3 = (bf16[3,1,160,384]{3,2,1,0:T(8,128)(2,1)S(1)}, bf16[3,1,160,384]{3,2,1,0:T(8,128)(2,1)S(1)}, u32[]{:S(2)}, u32[]{:S(2)}) collective-permute-start(bf16[3,1,160,384]{3,2,1,0:T(8,128)(2,1)S(1)} %get-tuple-element.40), channel_id=1, source_target_pairs={{4,0},{8,4},{12,8},{5,1},{9,5},{13,9},{6,2},{10,6},{14,10},{7,3},{... | collective-permute-start | bytes 1105928 | tf_op jit(solution)/shard_map/ppermute | solution.py:21
  32.6 3.9 %fusion.53 = (bf16[1,1,3,384,384]{4,3,2,1,0:T(8,128)(2,1)S(1)}, bf16[1,1,3,384,384]{4,3,2,1,0:T(8,128)(2,1)S(1)}, bf16[1,1,3,384,384]{4,3,2,1,0:T(8,128)(2,1)S(1...) fusion(bf16[3,3,3,384,384]{4,3,2,1,0:T(8,128)(2,1)} %param.19), kind=kLoop, calls=%fused_computation.96 | loop fusion | bytes 15925248 | tf_op jit(solution)/shard_map/slice | solution.py:41
  36.5 0.0 collective-permute-done.2
  36.5 0.1 collective-permute-done.3
  36.6 1.5 %select_maximum_fusion = bf16[3,5,162,384]{3,2,1,0:T(8,128)(2,1)S(1)} fusion(bf16[3,1,160,384]{3,2,1,0:T(8,128)(2,1)S(1)} %collective-permute-done.3, bf16[3,1,160,384]{3,2,1,0:T(8,128)(2,1)S(1)} %collective-permute-done.2, bf16[1,3,160,384]{3,2,1,0:T(8,128)(2,1)S(1)} %fusion.43, bf16[1,3,160,384]{3,2,1,0:T(8,128)(2,1)S(1)} %collective-permute-done.1, ...), kind=kLoop, calls=%fused_computation.10 | loop fusion | flops 16796160 | bytes 3709440 | tf_op jit(solution)/shard_map/concatenate | solution.py:22
  38.1 1.1 %fusion.54 = (bf16[1,3,160,384]{3,2,1,0:T(8,128)(2,1)S(1)}, bf16[1,3,160,384]{3,2,1,0:T(8,128)(2,1)S(1)}, bf16[1,3,160,384]{3,2,1,0:T(8,128)(2,1)S(1)}, bf16[1,3...) fusion(bf16[3,5,162,384]{3,2,1,0:T(8,128)(2,1)S(1)} %select_max, ...), kind=kLoop, calls=%fused_computation.97 | loop fusion | bytes 13271040 | tf_op jit(solution)/shard_map/slice | solution.py:38
  39.3 1.3 %fusion.26 = (bf16[1,3,160,1152]{3,2,1,0:T(8,128)(2,1)S(1)}, bf16[1,3,160,1152]{3,2,1,0:T(8,128)(2,1)S(1)}, bf16[1,3,160,1152]{3,2,1,0:T(8,128)(2,1)S(1)}) fusion(bf16[3,1,160,384]{3,2,1,0:T(8,128)(2,1)S(1)} %collective-permute-done.2, bf16[1,3,160,384]{3,2,1,0:T(8,128)(2,1)S(1)} %fusion.43, bf16[1,3,160,384]{3,2,1,0:T(8,128)(2,1)S(1)} %collective-permute-done.1, ...), kind=kLoop, calls=%fused_computation.41 | loop fusion | flops 19906560 | bytes 7004160 | tf_op jit(solution)/shard_map/concatenate | solution.py:37
  40.5 0.8 fusion.55
  41.3 0.1 pad_maximum_fusion.20
  41.4 0.2 pad_maximum_fusion.18
  41.6 0.8 convolution_add_fusion.10
  42.4 0.5 fusion.24
  43.0 0.8 convolution_add_fusion.9
  43.7 0.8 convolution_add_fusion.8
  44.5 0.8 convolution_add_fusion.7
  45.3 0.8 convolution_add_fusion.6
  46.0 0.8 convolution_add_fusion.5
  46.8 0.8 convolution_add_fusion.4
  47.6 0.0 copy-start.2
  47.6 0.0 copy-start.3
  47.6 0.0 copy-start.4
  47.6 0.0 copy-start.5
  47.6 0.8 convolution_add_fusion.3
  48.4 0.0 copy-start.7
  48.4 0.0 copy-start.10
  48.4 0.1 copy-done.2
  48.6 0.0 copy-done.3
  48.6 0.2 fusion.44
  48.8 0.0 copy-done.4
  48.8 0.0 copy-done.5
  48.8 0.9 fusion.47
  49.7 0.0 all-gather.2.cloned.1.call-update
  49.8 0.0 copy-done.7
  49.8 0.0 copy-done.10
  49.8 1.4 %fusion.14 = bf16[480,384]{1,0:T(8,128)(2,1)S(1)} fusion(bf16[480,384]{1,0:T(8,128)(2,1)} %bitcast.75, bf16[384,384]{1,0:T(8,128)(2,1)S(1)} %copy-done.7, f32[384]{0:T(512)S(1)} %copy-done.10), kind=kOutput, calls=%fused_computation.31 | convolution fusion | flops 141926400 | bytes 1033728 | tf_op jit(solution)/shard_map/dot_general | solution.py:92
  51.2 32.2 %all-gather.2.cloned.1.call-done = bf16[1,12,160,384]{3,2,0,1:T(8,128)(2,1)} async-done(((bf16[1,3,160,384]{3,2,0,1:T(8,128)(2,1)}), bf16[1,12,160,384]{3,2,0,1:T(8,128)(2,1)}) %all-gather.2.cloned.1.call-update) | async-done | bytes 1474576 | tf_op jit(solution)/shard_map/all_gather | solution.py:100
  83.3 0.0 copy-done
  83.3 0.0 copy-start.6
  83.3 0.0 copy-start.8
  83.3 0.0 copy-start.11
  83.4 5.3 %multiply_reduce_fusion = (f32[480]{0:T(512)S(1)}, f32[480,1920]{1,0:T(8,128)}) fusion(bf16[480,384]{1,0:T(8,128)(2,1)S(1)} %fusion.14, bf16[1920,384]{1,0:T(8,128)(2,1)} %bitcast.79, bf16[384,384]{1,0:T(8,128)(2,1)S(1)} %copy-done), kind=kOutput, calls=%fused_computation.4 | convolution fusion | flops 1276599808 | bytes 5826432 | tf_op jit(solution)/shard_map/fqc,fkc->fqk/dot_general | solution.py:49
  88.7 0.0 copy-done.6
  88.7 0.0 copy-done.8
  88.7 0.0 copy-done.11
  88.7 0.0 copy-start.1
  88.7 2.2 %fusion.3 = bf16[1920,384]{1,0:T(8,128)(2,1)} fusion(bf16[1920,384]{1,0:T(8,128)(2,1)S(1)} %bitcast.80, bf16[384,384]{1,0:T(8,128)(2,1)S(1)} %copy-done.8, f32[384]{0:T(512)S(1)} %copy-done.11), kind=kOutput, calls=%fused_computation.9 | convolution fusion | flops 567705600 | bytes 3245568 | tf_op jit(solution)/shard_map/dot_general | solution.py:103
  90.9 0.0 copy-start.9
  90.9 0.0 copy-done.1
  90.9 0.7 fusion.1
  91.7 0.2 copy-done.9
  91.9 0.0 copy-done.12
  91.9 0.5 copy-done.13
  92.4 3.5 %convolution_add_fusion.1 = f32[480,384]{1,0:T(8,128)S(1)} fusion(bf16[384,384]{1,0:T(8,128)(2,1)S(1)} %copy-done.9, bf16[1920,384]{1,0:T(8,128)(2,1)S(1)} %copy-done.13, f32[480,1920]{1,0:T(8,128)} %get-tuple-element.43, f32[480]{0:T(512)S(1)} %broadcast_maximum_fusion, f32[384]{0:T(512)S(1)} %copy-done.12, f32[480]{0:T(512)S(1)} %fusion.1), kind=kOutput, calls=%fused_computation.21 | convolution fusion | flops 852664320 | bytes 6198528 | tf_op jit(solution)/shard_map/dot_general | solution.py:107
  96.0 0.8 fusion.49
  (5 shorter events, 0.0 us)
Async XLA Ops:
  6.5 76.8 %copy-start = (bf16[384,384]{1,0:T(8,128)(2,1)S(1)}, bf16[384,384]{1,0:T(8,128)(2,1)}, u32[]{:S(2)}) copy-start(bf16[384,384]{1,0:T(8,128)(2,1)} %param.25) | copy-start | bytes 884740
  6.5 76.8 %all-gather.2.cloned.1.call-start = ((), (), s32[]{:S(2)}) async-start(), calls=%async_computation | async-start | bytes 1843200 | tf_op jit(solution)/shard_map/all_gather | solution.py:100
  9.1 13.9 %collective-permute-start.1 = (bf16[1,3,160,384]{3,2,1,0:T(8,128)(2,1)S(1)}, bf16[1,3,160,384]{3,2,1,0:T(8,128)(2,1)S(1)}, u32[]{:S(2)}, u32[]{:S(2)}) collective-permute-start(bf16[1,3,160,384]{3,2,1,0:T(8,128)(2,1)S(1)} %fusion.43), channel_id=1, source_target_pairs={{0,1},{1,2},{2,3},{4,5},{5,6},{6,7},{8,9},{9,10},{10,11},{12,13},{... | collective-permute-start | bytes 1105928 | tf_op jit(solution)/shard_map/ppermute | solution.py:10
  14.1 15.8 %collective-permute-start = (bf16[1,3,160,384]{3,2,1,0:T(8,128)(2,1)S(1)}, bf16[1,3,160,384]{3,2,1,0:T(8,128)(2,1)S(1)}, u32[]{:S(2)}, u32[]{:S(2)}) collective-permute-start(bf16[1,3,160,384]{3,2,1,0:T(8,128)(2,1)S(1)} %fusion.43), channel_id=1, source_target_pairs={{0,2},{1,3},{4,6},{5,7},{8,10},{9,11},{12,14},{13,15},{16,18},{17,... | collective-permute-start | bytes 1105928 | tf_op jit(solution)/shard_map/ppermute | solution.py:10
  29.9 6.6 %collective-permute-start.2 = (bf16[3,1,160,384]{3,2,1,0:T(8,128)(2,1)S(1)}, bf16[3,1,160,384]{3,2,1,0:T(8,128)(2,1)S(1)}, u32[]{:S(2)}, u32[]{:S(2)}) collective-permute-start(bf16[3,1,160,384]{3,2,1,0:T(8,128)(2,1)S(1)} %get-tuple-element.41), channel_id=1, source_target_pairs={{0,4},{4,8},{8,12},{1,5},{5,9},{9,13},{2,6},{6,10},{10,14},{3,7},{... | collective-permute-start | bytes 1105928 | tf_op jit(solution)/shard_map/ppermute | solution.py:20
  31.3 5.3 %collective-permute-start.3 = (bf16[3,1,160,384]{3,2,1,0:T(8,128)(2,1)S(1)}, bf16[3,1,160,384]{3,2,1,0:T(8,128)(2,1)S(1)}, u32[]{:S(2)}, u32[]{:S(2)}) collective-permute-start(bf16[3,1,160,384]{3,2,1,0:T(8,128)(2,1)S(1)} %get-tuple-element.40), channel_id=1, source_target_pairs={{4,0},{8,4},{12,8},{5,1},{9,5},{13,9},{6,2},{10,6},{14,10},{7,3},{... | collective-permute-start | bytes 1105928 | tf_op jit(solution)/shard_map/ppermute | solution.py:21
  47.6 1.0 copy-start.2
  47.6 1.0 copy-start.3
  47.6 1.2 %copy-start.4 = (f32[384]{0:T(512)S(1)}, f32[384]{0:T(512)}, u32[]{:S(2)}) copy-start(f32[384]{0:T(512)} %param.22) | copy-start | bytes 4612
  47.6 1.2 %copy-start.5 = (f32[384]{0:T(512)S(1)}, f32[384]{0:T(512)}, u32[]{:S(2)}) copy-start(f32[384]{0:T(512)} %param.21) | copy-start | bytes 4612
  48.4 1.4 %copy-start.7 = (bf16[384,384]{1,0:T(8,128)(2,1)S(1)}, bf16[384,384]{1,0:T(8,128)(2,1)}, u32[]{:S(2)}) copy-start(bf16[384,384]{1,0:T(8,128)(2,1)} %param.23) | copy-start | bytes 884740
  48.4 1.4 %copy-start.10 = (f32[384]{0:T(512)S(1)}, f32[384]{0:T(512)}, u32[]{:S(2)}) copy-start(f32[384]{0:T(512)} %param.24) | copy-start | bytes 4612
  83.3 5.4 %copy-start.6 = (bf16[1,12,160,384]{3,2,0,1:T(8,128)(2,1)S(1)}, bf16[1,12,160,384]{3,2,0,1:T(8,128)(2,1)}, u32[]{:S(2)}) copy-start(bf16[1,12,160,384]{3,2,0,1:T(8,128)(2,1)} %all-gather.2.cloned.1.call-done) | copy-start | bytes 4423684
  83.3 5.4 %copy-start.8 = (bf16[384,384]{1,0:T(8,128)(2,1)S(1)}, bf16[384,384]{1,0:T(8,128)(2,1)}, u32[]{:S(2)}) copy-start(bf16[384,384]{1,0:T(8,128)(2,1)} %param.26) | copy-start | bytes 884740
  83.3 5.4 %copy-start.11 = (f32[384]{0:T(512)S(1)}, f32[384]{0:T(512)}, u32[]{:S(2)}) copy-start(f32[384]{0:T(512)} %param.27) | copy-start | bytes 4612
  88.7 2.2 %copy-start.1 = (f32[480,1920]{1,0:T(8,128)S(1)}, f32[480,1920]{1,0:T(8,128)}, u32[]{:S(2)}) copy-start(f32[480,1920]{1,0:T(8,128)} %get-tuple-element.43) | copy-start | bytes 11059204
  90.9 1.0 copy-start.9
  90.9 1.0 copy-start.12
  90.9 1.5 %copy-start.13 = (bf16[1920,384]{1,0:T(8,128)(2,1)S(1)}, bf16[1920,384]{1,0:T(8,128)(2,1)}, u32[]{:S(2)}) copy-start(bf16[1920,384]{1,0:T(8,128)(2,1)} %fusion.3) | copy-start | bytes 4423684
Sparse Core Ops, SparseCore 0:
  49.9 33.4 all-gather.1
where the time goes:
time: 104 us
  waiting for transfers between devices  43.5 us (42%)
  matrix products  19.3 us (19%)
  between operations  13.7 us (13%)
  starting transfers between devices  12.1 us (12%)
  other arithmetic  9.02 us (9%)
  local copies, waits for them, and re-layouts  6.02 us (6%)
    all_gather x1, waiting for transfers between devices, shards(): lax.all_gather(normed, 'space', axis=1, tiled=True)  32.2 us
    ppermute x2, waiting for transfers between devices, from_behind(): lax.ppermute(value, axis, [(source, source + steps) for source in range(l...  11.2 us
    ppermute x2, starting transfers between devices, from_behind(): lax.ppermute(value, axis, [(source, source + steps) for source in range(l...  9.48 us
    dot_general x9, matrix products, causal_conv(): jnp.dot(joined, kernel, preferred_element_type=jnp.float32)  6.87 us
    dot_general x1, matrix products, absorb(): jnp.einsum('fqc,fkc->fqk', queries, key_rows, preferred_element_type=jnp....  5.34 us
    slice x1, local copies, waits for them, and re-layouts, causal_conv(): kernel = conv_weight[tap_t, tap_y].reshape(3 * channels, channels)  3.94 us
    dot_general x1, matrix products, shards(): jnp.dot(attended, out_weight, preferred_element_type=jnp.float32) + out_bias  3.54 us
    dot_general x1, matrix products, shards(): jnp.dot(source, value_weight, preferred_element_type=jnp.float32)  2.19 us
  transfers between devices with their start and end apart: 5, of which 4 were waited for; matrix products, arithmetic and copies ran while one was open for 5% of the time, Pallas kernels for 0%

commit v1 on v0

--- a/solution.py
+++ b/solution.py
@@ -2,6 +2,22 @@
 import jax.numpy as jnp
 from jax import lax
 from jax.sharding import PartitionSpec as P
+
+
+def _guide_classes(raw):
+    m_next, mat_out, res = (lax.axis_size("space"), lax.axis_index("space"), raw.shape[1])
+    lower = lax.dynamic_update_slice_in_dim(
+        jnp.zeros([h * m_next if num == 1 else h for num, h in enumerate(raw.shape)], raw.dtype),
+        raw,
+        mat_out * res,
+        axis=1,
+    )
+    no = 1
+    while no < m_next:
+        raw = lax.ppermute(raw, "space", [(num, (num + 1) % m_next) for num in range(m_next)])
+        lower = lax.dynamic_update_slice_in_dim(lower, raw, (mat_out - no) % m_next * res, axis=1)
+        no += 1
+    return lower
 
 
 def from_behind(value, axis, steps):
@@ -97,7 +113,7 @@
         jnp.zeros((frame_count, query_count), jnp.float32),
         jnp.full((frame_count, query_count), -1e30, jnp.float32),
     )
-    source = lax.all_gather(normed, "space", axis=1, tiled=True).reshape(frame_count, -1, channels)
+    source = _guide_classes(normed).reshape(frame_count, -1, channels)
     key_rows = jnp.dot(source, key_weight, preferred_element_type=jnp.float32).astype(jnp.bfloat16)
     value_rows = (
         jnp.dot(source, value_weight, preferred_element_type=jnp.float32) + value_bias

time: 104 us -> 88.3 us (0.85)
  the two profiles are of different devices: /device:TPU:0 before, /device:TPU:22 now
where the time goes in v1:
time: 88.3 us; the launch traced here: 88.1 us
  waiting for transfers between devices  44.9 us (51%)
  matrix products  16.4 us (19%)
  starting transfers between devices  10.4 us (12%)
  other arithmetic  10.2 us (12%)
  local copies, waits for them, and re-layouts  5.76 us (7%)
    ppermute x2, waiting for transfers between devices, from_behind(): lax.ppermute(value, axis, [(source, source + steps) for source in range(l...  24.2 us
    ppermute x3, waiting for transfers between devices, _guide_classes(): lax.ppermute(raw, 'space', [(num, (num + 1) % m_next) for num in range(m_...  19.7 us
    dot_general x9, matrix products, causal_conv(): jnp.dot(joined, kernel, preferred_element_type=jnp.float32)  6.84 us
    ppermute x2, starting transfers between devices, from_behind(): lax.ppermute(value, axis, [(source, source + steps) for source in range(l...  4.78 us
    dot_general x1, matrix products, absorb(): jnp.einsum('fqk,fkc->fqc', weights, value_rows, preferred_element_type=jn...  4.16 us
    slice x1, local copies, waits for them, and re-layouts, causal_conv(): kernel = conv_weight[tap_t, tap_y].reshape(3 * channels, channels)  3.92 us
    dot_general x1, matrix products, absorb(): jnp.einsum('fqc,fkc->fqk', queries, key_rows, preferred_element_type=jnp....  3.88 us
    ppermute x1, starting transfers between devices, padded_2(): after = lax.ppermute(leading, axis, down)  3.64 us
  transfers between devices with their start and end apart: 7, of which 6 were waited for; matrix products, arithmetic and copies ran while one was open for 6% of the time, Pallas kernels for 0%

profile of v1, /device:TPU:22, one launch (start us, length us, event | category | flops | bytes accessed | tf_op | source)
XLA Modules:
  0.0 88.1 jit_solution(12622373397800710593)
XLA Ops:
  0.0 0.0 copy-start
  0.0 1.2 %fusion.33 = f32[3,160]{1,0:T(4,128)S(1)} fusion(bf16[1,3,160,384]{3,2,1,0:T(8,128)(2,1)} %param.16), kind=kLoop, calls=%fused_computation.72 | loop fusion | flops 552480 | bytes 370560 | tf_op jit(solution)/shard_map/reduce_sum | solution.py:43
  1.2 1.3 %fusion.41 = bf16[1,3,160,384]{3,2,1,0:T(8,128)(2,1)S(1)} fusion(bf16[1,3,160,384]{3,2,1,0:T(8,128)(2,1)} %param.16, f32[384]{0:T(512)} %param.18, f32[384]{0:T(512)} %param.17, f32[3,160]{1,0:T(4,128)S(1)} %add_rsqrt_fusion.1), kind=kLoop, calls=%fused_computation.80 | loop fusion | flops 1658880 | bytes 742272 | tf_op jit(solution)/shard_map/convert_element_type | solution.py:96
  2.6 1.3 %collective-permute-start = (bf16[1,3,160,384]{3,2,1,0:T(8,128)(2,1)S(1)}, bf16[1,3,160,384]{3,2,1,0:T(8,128)(2,1)S(1)}, u32[]{:S(2)}, u32[]{:S(2)}) collective-permute-start(bf16[1,3,160,384]{3,2,1,0:T(8,128)(2,1)S(1)} %fusion.41), channel_id=1, source_target_pairs={{0,2},{1,3},{4,6},{5,7},{8,10},{9,11},{12,14},{13,15},{16,18},{17,... | collective-permute-start | bytes 1105928 | tf_op jit(solution)/shard_map/ppermute | solution.py:26
  3.9 3.5 %collective-permute-start.1 = (bf16[1,3,160,384]{3,2,1,0:T(8,128)(2,1)S(1)}, bf16[1,3,160,384]{3,2,1,0:T(8,128)(2,1)S(1)}, u32[]{:S(2)}, u32[]{:S(2)}) collective-permute-start(bf16[1,3,160,384]{3,2,1,0:T(8,128)(2,1)S(1)} %fusion.41), channel_id=1, source_target_pairs={{0,1},{1,2},{2,3},{4,5},{5,6},{6,7},{8,9},{9,10},{10,11},{12,13},{... | collective-permute-start | bytes 1105928 | tf_op jit(solution)/shard_map/ppermute | solution.py:26
  7.4 9.5 %collective-permute-done = bf16[1,3,160,384]{3,2,1,0:T(8,128)(2,1)S(1)} collective-permute-done((bf16[1,3,160,384]{3,2,1,0:T(8,128)(2,1)S(1)}, bf16[1,3,160,384]{3,2,1,0:T(8,128)(2,1)S(1)}, u32[]{:S(2)}, u32[]{:S(2)}) %collective-permute-start) | collective-permute-done | bytes 368672 | tf_op jit(solution)/shard_map/ppermute | solution.py:26
  16.9 14.7 %collective-permute-done.1 = bf16[1,3,160,384]{3,2,1,0:T(8,128)(2,1)S(1)} collective-permute-done((bf16[1,3,160,384]{3,2,1,0:T(8,128)(2,1)S(1)}, bf16[1,3,160,384]{3,2,1,0:T(8,128)(2,1)S(1)}, u32[]{:S(2)}, u32[]{:S(2)}) %collective-permute-start.1) | collective-permute-done | bytes 368672 | tf_op jit(solution)/shard_map/ppermute | solution.py:26
  31.5 0.1 pad_maximum_fusion.21
  31.6 1.9 %collective-permute-start.2 = (bf16[3,1,160,384]{3,2,1,0:T(8,128)(2,1)S(1)}, bf16[3,1,160,384]{3,2,1,0:T(8,128)(2,1)S(1)}, u32[]{:S(2)}, u32[]{:S(2)}) collective-permute-start(bf16[3,1,160,384]{3,2,1,0:T(8,128)(2,1)S(1)} %get-tuple-element.43), channel_id=1, source_target_pairs={{0,4},{4,8},{8,12},{1,5},{5,9},{9,13},{2,6},{6,10},{10,14},{3,7},{... | collective-permute-start | bytes 1105928 | tf_op jit(solution)/shard_map/ppermute | solution.py:36
  33.6 3.6 %collective-permute-start.3 = (bf16[3,1,160,384]{3,2,1,0:T(8,128)(2,1)S(1)}, bf16[3,1,160,384]{3,2,1,0:T(8,128)(2,1)S(1)}, u32[]{:S(2)}, u32[]{:S(2)}) collective-permute-start(bf16[3,1,160,384]{3,2,1,0:T(8,128)(2,1)S(1)} %get-tuple-element.42), channel_id=1, source_target_pairs={{4,0},{8,4},{12,8},{5,1},{9,5},{13,9},{6,2},{10,6},{14,10},{7,3},{... | collective-permute-start | bytes 1105928 | tf_op jit(solution)/shard_map/ppermute | solution.py:37
  37.2 3.9 %fusion.49 = (bf16[1,1,3,384,384]{4,3,2,1,0:T(8,128)(2,1)S(1)}, bf16[1,1,3,384,384]{4,3,2,1,0:T(8,128)(2,1)S(1)}, bf16[1,1,3,384,384]{4,3,2,1,0:T(8,128)(2,1)S(1...) fusion(bf16[3,3,3,384,384]{4,3,2,1,0:T(8,128)(2,1)} %param.19), kind=kLoop, calls=%fused_computation.98 | loop fusion | bytes 15925248 | tf_op jit(solution)/shard_map/slice | solution.py:57
  41.1 0.0 collective-permute-done.2
  41.1 1.1 %collective-permute-done.3 = bf16[3,1,160,384]{3,2,1,0:T(8,128)(2,1)S(1)} collective-permute-done((bf16[3,1,160,384]{3,2,1,0:T(8,128)(2,1)S(1)}, bf16[3,1,160,384]{3,2,1,0:T(8,128)(2,1)S(1)}, u32[]{:S(2)}, u32[]{:S(2)}) %collective-permute-start.3) | collective-permute-done | bytes 368672 | tf_op jit(solution)/shard_map/ppermute | solution.py:37
  42.2 1.5 %select_maximum_fusion = bf16[3,5,162,384]{3,2,1,0:T(8,128)(2,1)S(1)} fusion(bf16[3,1,160,384]{3,2,1,0:T(8,128)(2,1)S(1)} %collective-permute-done.3, bf16[3,1,160,384]{3,2,1,0:T(8,128)(2,1)S(1)} %collective-permute-done.2, bf16[1,3,160,384]{3,2,1,0:T(8,128)(2,1)S(1)} %fusion.41, bf16[1,3,160,384]{3,2,1,0:T(8,128)(2,1)S(1)} %collective-permute-done.1, ...), kind=kLoop, calls=%fused_computation.10 | loop fusion | flops 16796160 | bytes 3709440 | tf_op jit(solution)/shard_map/concatenate | solution.py:38
  43.8 1.1 %fusion.50 = (bf16[1,3,160,384]{3,2,1,0:T(8,128)(2,1)S(1)}, bf16[1,3,160,384]{3,2,1,0:T(8,128)(2,1)S(1)}, bf16[1,3,160,384]{3,2,1,0:T(8,128)(2,1)S(1)}, bf16[1,3...) fusion(bf16[3,5,162,384]{3,2,1,0:T(8,128)(2,1)S(1)} %select_max, ...), kind=kLoop, calls=%fused_computation.99 | loop fusion | bytes 13271040 | tf_op jit(solution)/shard_map/slice | solution.py:54
  44.9 1.3 %fusion.18 = (bf16[1,3,160,1152]{3,2,1,0:T(8,128)(2,1)S(1)}, bf16[1,3,160,1152]{3,2,1,0:T(8,128)(2,1)S(1)}, bf16[1,3,160,1152]{3,2,1,0:T(8,128)(2,1)S(1)}) fusion(bf16[3,1,160,384]{3,2,1,0:T(8,128)(2,1)S(1)} %collective-permute-done.2, bf16[1,3,160,384]{3,2,1,0:T(8,128)(2,1)S(1)} %fusion.41, bf16[1,3,160,384]{3,2,1,0:T(8,128)(2,1)S(1)} %collective-permute-done.1, ...), kind=kLoop, calls=%fused_computation.39 | loop fusion | flops 19906560 | bytes 7004160 | tf_op jit(solution)/shard_map/concatenate | solution.py:53
  46.2 0.8 fusion.51
  46.9 0.1 pad_maximum_fusion.20
  47.1 0.2 pad_maximum_fusion.18
  47.3 0.8 convolution_add_fusion.10
  48.1 0.4 fusion.16
  48.4 0.8 convolution_add_fusion.9
  49.2 0.8 convolution_add_fusion.8
  50.0 0.8 convolution_add_fusion.7
  50.7 0.8 convolution_add_fusion.6
  51.5 0.8 convolution_add_fusion.5
  52.3 0.8 convolution_add_fusion.4
  53.0 0.0 copy-start.1
  53.1 0.0 copy-start.3
  53.1 0.8 convolution_add_fusion.3
  53.8 0.0 copy-start.4
  53.9 0.0 copy-start.5
  53.9 0.2 copy-done.1
  54.0 0.0 copy-done.3
  54.0 0.2 fusion.42
  54.3 0.1 broadcast_in_dim.4
  54.4 0.1 copy-done.4
  54.6 0.0 copy-done.5
  54.6 0.2 constant_dynamic-update-slice_fusion.3
  54.8 0.1 collective-permute-start.4
  54.9 7.1 %collective-permute-done.4 = bf16[1,3,160,384]{3,2,1,0:T(8,128)(2,1)S(1)} collective-permute-done((bf16[1,3,160,384]{3,2,1,0:T(8,128)(2,1)S(1)}, bf16[1,3,160,384]{3,2,1,0:T(8,128)(2,1)S(1)}, u32[]{:S(2)}, u32[]{:S(2)}) %collective-permute-start.4) | collective-permute-done | bytes 368672 | tf_op jit(solution)/shard_map/ppermute | solution.py:17
  62.0 0.0 collective-permute-start.5
  62.0 6.9 %collective-permute-done.5 = bf16[1,3,160,384]{3,2,1,0:T(8,128)(2,1)S(1)} collective-permute-done((bf16[1,3,160,384]{3,2,1,0:T(8,128)(2,1)S(1)}, bf16[1,3,160,384]{3,2,1,0:T(8,128)(2,1)S(1)}, u32[]{:S(2)}, u32[]{:S(2)}) %collective-permute-start.5) | collective-permute-done | bytes 368672 | tf_op jit(solution)/shard_map/ppermute | solution.py:17
  68.9 0.0 collective-permute-start.6
  68.9 0.0 copy-done.7
  68.9 0.0 copy-done.9
  68.9 1.1 %fusion.14 = bf16[480,384]{1,0:T(8,128)(2,1)} fusion(bf16[480,384]{1,0:T(8,128)(2,1)S(1)} %bitcast.71, bf16[384,384]{1,0:T(8,128)(2,1)S(1)} %copy-done.7, f32[384]{0:T(512)S(1)} %copy-done.9), kind=kOutput, calls=%fused_computation.31 | convolution fusion | flops 141926400 | bytes 1033728 | tf_op jit(solution)/shard_map/dot_general | solution.py:108
  70.0 0.1 constant_dynamic-update-slice_fusion.2
  70.1 0.1 constant_dynamic-update-slice_fusion.1
  70.2 5.7 %collective-permute-done.6 = bf16[1,3,160,384]{3,2,1,0:T(8,128)(2,1)S(1)} collective-permute-done((bf16[1,3,160,384]{3,2,1,0:T(8,128)(2,1)S(1)}, bf16[1,3,160,384]{3,2,1,0:T(8,128)(2,1)S(1)}, u32[]{:S(2)}, u32[]{:S(2)}) %collective-permute-start.6) | collective-permute-done | bytes 368672 | tf_op jit(solution)/shard_map/ppermute | solution.py:17
  75.8 0.1 constant_dynamic-update-slice_fusion
  75.9 0.0 copy-done
  75.9 0.0 copy-done.11
  75.9 3.9 %multiply_reduce_fusion = (f32[480]{0:T(512)S(1)}, f32[480,1920]{1,0:T(8,128)}) fusion(bf16[480,384]{1,0:T(8,128)(2,1)S(1)} %copy-done.11, bf16[1920,384]{1,0:T(8,128)(2,1)S(1)} %bitcast.67, bf16[384,384]{1,0:T(8,128)(2,1)S(1)} %copy-done), kind=kOutput, calls=%fused_computation.4 | convolution fusion | flops 1276599808 | bytes 5826432 | tf_op jit(solution)/shard_map/fqc,fkc->fqk/dot_general | solution.py:65
  79.8 2.8 %fusion.1 = f32[480]{0:T(512)S(1)} fusion(f32[480,1920]{1,0:T(8,128)} %get-tuple-element.45, f32[480]{0:T(512)S(1)} %broadcast_maximum_fusion), kind=kLoop, calls=%fused_computation.5 | loop fusion | flops 2764320 | bytes 3690240 | tf_op jit(solution)/shard_map/reduce_sum | solution.py:73
  82.6 0.0 copy-done.8
  82.6 0.0 copy-done.10
  82.7 0.0 copy-start.2
  82.7 0.0 copy-start.6
  82.7 4.2 %fusion.30 = bf16[480,384]{1,0:T(8,128)(2,1)S(1)} fusion(bf16[1920,384]{1,0:T(8,128)(2,1)S(1)} %bitcast.68, bf16[384,384]{1,0:T(8,128)(2,1)S(1)} %copy-done.8, f32[384]{0:T(512)S(1)} %copy-done.10, f32[480,1920]{1,0:T(8,128)} %get-tuple-element.45, f32[480]{0:T(512)S(1)} %broadcast_maximum_fusion, f32[480]{0:T(512)S(1)} %fusion.1), kind=kOutput, calls=%fused_computation.69 | convolution fusion | flops 1278627840 | bytes 5829888 | tf_op jit(solution)/shard_map/fqk,fkc->fqc/dot_general | solution.py:71
  86.8 0.0 copy-done.2
  86.9 0.0 copy-done.6
  86.9 0.4 convolution_add_fusion.1
  87.3 0.8 fusion.46
  (8 shorter events, 0.0 us)
Async XLA Ops:
  0.0 75.9 %copy-start = (bf16[384,384]{1,0:T(8,128)(2,1)S(1)}, bf16[384,384]{1,0:T(8,128)(2,1)}, u32[]{:S(2)}) copy-start(bf16[384,384]{1,0:T(8,128)(2,1)} %param.25) | copy-start | bytes 884740
  2.6 14.3 %collective-permute-start = (bf16[1,3,160,384]{3,2,1,0:T(8,128)(2,1)S(1)}, bf16[1,3,160,384]{3,2,1,0:T(8,128)(2,1)S(1)}, u32[]{:S(2)}, u32[]{:S(2)}) collective-permute-start(bf16[1,3,160,384]{3,2,1,0:T(8,128)(2,1)S(1)} %fusion.41), channel_id=1, source_target_pairs={{0,2},{1,3},{4,6},{5,7},{8,10},{9,11},{12,14},{13,15},{16,18},{17,... | collective-permute-start | bytes 1105928 | tf_op jit(solution)/shard_map/ppermute | solution.py:26
  3.9 27.7 %collective-permute-start.1 = (bf16[1,3,160,384]{3,2,1,0:T(8,128)(2,1)S(1)}, bf16[1,3,160,384]{3,2,1,0:T(8,128)(2,1)S(1)}, u32[]{:S(2)}, u32[]{:S(2)}) collective-permute-start(bf16[1,3,160,384]{3,2,1,0:T(8,128)(2,1)S(1)} %fusion.41), channel_id=1, source_target_pairs={{0,1},{1,2},{2,3},{4,5},{5,6},{6,7},{8,9},{9,10},{10,11},{12,13},{... | collective-permute-start | bytes 1105928 | tf_op jit(solution)/shard_map/ppermute | solution.py:26
  31.6 9.5 %collective-permute-start.2 = (bf16[3,1,160,384]{3,2,1,0:T(8,128)(2,1)S(1)}, bf16[3,1,160,384]{3,2,1,0:T(8,128)(2,1)S(1)}, u32[]{:S(2)}, u32[]{:S(2)}) collective-permute-start(bf16[3,1,160,384]{3,2,1,0:T(8,128)(2,1)S(1)} %get-tuple-element.43), channel_id=1, source_target_pairs={{0,4},{4,8},{8,12},{1,5},{5,9},{9,13},{2,6},{6,10},{10,14},{3,7},{... | collective-permute-start | bytes 1105928 | tf_op jit(solution)/shard_map/ppermute | solution.py:36
  33.6 8.7 %collective-permute-start.3 = (bf16[3,1,160,384]{3,2,1,0:T(8,128)(2,1)S(1)}, bf16[3,1,160,384]{3,2,1,0:T(8,128)(2,1)S(1)}, u32[]{:S(2)}, u32[]{:S(2)}) collective-permute-start(bf16[3,1,160,384]{3,2,1,0:T(8,128)(2,1)S(1)} %get-tuple-element.42), channel_id=1, source_target_pairs={{4,0},{8,4},{12,8},{5,1},{9,5},{13,9},{6,2},{10,6},{14,10},{7,3},{... | collective-permute-start | bytes 1105928 | tf_op jit(solution)/shard_map/ppermute | solution.py:37
  53.0 1.0 %copy-start.1 = (bf16[1,3,160,384]{3,2,1,0:T(8,128)(2,1)S(1)}, bf16[1,3,160,384]{3,2,1,0:T(8,128)(2,1)}, u32[]{:S(2)}) copy-start(bf16[1,3,160,384]{3,2,1,0:T(8,128)(2,1)} %param.15) | copy-start | bytes 1105924
  53.1 1.0 %copy-start.3 = (f32[384]{0:T(512)S(1)}, f32[384]{0:T(512)}, u32[]{:S(2)}) copy-start(f32[384]{0:T(512)} %param.20) | copy-start | bytes 4612
  53.8 0.7 copy-start.4
  53.9 0.7 copy-start.5
  54.0 14.9 %copy-start.7 = (bf16[384,384]{1,0:T(8,128)(2,1)S(1)}, bf16[384,384]{1,0:T(8,128)(2,1)}, u32[]{:S(2)}) copy-start(bf16[384,384]{1,0:T(8,128)(2,1)} %param.23) | copy-start | bytes 884740
  54.0 14.9 %copy-start.9 = (f32[384]{0:T(512)S(1)}, f32[384]{0:T(512)}, u32[]{:S(2)}) copy-start(f32[384]{0:T(512)} %param.24) | copy-start | bytes 4612
  54.8 7.2 %collective-permute-start.4 = (bf16[1,3,160,384]{3,2,1,0:T(8,128)(2,1)S(1)}, bf16[1,3,160,384]{3,2,1,0:T(8,128)(2,1)S(1)}, u32[]{:S(2)}, u32[]{:S(2)}) collective-permute-start(bf16[1,3,160,384]{3,2,1,0:T(8,128)(2,1)S(1)} %get-tuple-element.6), channel_id=1, source_target_pairs={{0,4},{4,8},{8,12},{12,0},{1,5},{5,9},{9,13},{13,1},{2,6},{6,10},{... | collective-permute-start | bytes 1105928 | tf_op jit(solution)/shard_map/ppermute | solution.py:17
  62.0 6.9 %collective-permute-start.5 = (bf16[1,3,160,384]{3,2,1,0:T(8,128)(2,1)S(1)}, bf16[1,3,160,384]{3,2,1,0:T(8,128)(2,1)S(1)}, u32[]{:S(2)}, u32[]{:S(2)}) collective-permute-start(bf16[1,3,160,384]{3,2,1,0:T(8,128)(2,1)S(1)} %collective-permute-done.4), channel_id=1, source_target_pairs={{0,4},{4,8},{8,12},{12,0},{1,5},{5,9},{9,13},{13,1},{2,6},{6,10},{... | collective-permute-start | bytes 1105928 | tf_op jit(solution)/shard_map/ppermute | solution.py:17
  68.9 6.9 %collective-permute-start.6 = (bf16[1,3,160,384]{3,2,1,0:T(8,128)(2,1)S(1)}, bf16[1,3,160,384]{3,2,1,0:T(8,128)(2,1)S(1)}, u32[]{:S(2)}, u32[]{:S(2)}) collective-permute-start(bf16[1,3,160,384]{3,2,1,0:T(8,128)(2,1)S(1)} %collective-permute-done.5), channel_id=1, source_target_pairs={{0,4},{4,8},{8,12},{12,0},{1,5},{5,9},{9,13},{13,1},{2,6},{6,10},{... | collective-permute-start | bytes 1105928 | tf_op jit(solution)/shard_map/ppermute | solution.py:17
  70.0 5.9 %copy-start.11 = (bf16[480,384]{1,0:T(8,128)(2,1)S(1)}, bf16[480,384]{1,0:T(8,128)(2,1)}, u32[]{:S(2)}) copy-start(bf16[480,384]{1,0:T(8,128)(2,1)} %fusion.14) | copy-start | bytes 1105924
  79.8 2.8 %copy-start.8 = (bf16[384,384]{1,0:T(8,128)(2,1)S(1)}, bf16[384,384]{1,0:T(8,128)(2,1)}, u32[]{:S(2)}) copy-start(bf16[384,384]{1,0:T(8,128)(2,1)} %param.26) | copy-start | bytes 884740
  79.8 2.8 %copy-start.10 = (f32[384]{0:T(512)S(1)}, f32[384]{0:T(512)}, u32[]{:S(2)}) copy-start(f32[384]{0:T(512)} %param.27) | copy-start | bytes 4612
  82.7 4.2 %copy-start.2 = (bf16[384,384]{1,0:T(8,128)(2,1)S(1)}, bf16[384,384]{1,0:T(8,128)(2,1)}, u32[]{:S(2)}) copy-start(bf16[384,384]{1,0:T(8,128)(2,1)} %param.28) | copy-start | bytes 884740
  82.7 4.2 %copy-start.6 = (f32[384]{0:T(512)S(1)}, f32[384]{0:T(512)}, u32[]{:S(2)}) copy-start(f32[384]{0:T(512)} %param.29) | copy-start | bytes 4612
